TPU v7x, 32 devices: a whole 2x2x4 slice. The times are simulated.
32 devices in a mesh: row: 8 (over z, x), col: 4 (over y, core).
Axes of the slice: x: 2, y: 2, z: 4, core: 2. Of those that a mesh axis runs over, the one named last changes fastest.
Arguments:
- krylov_block: bfloat16 [64, 16384], P(None, ('row', 'col')), may hold values from -54 to 54
- degree: int32 [16384], P(('row', 'col')), may hold values from 16 to 64
- tile_values: bfloat16 [256, 4, 64, 512], P('row', 'col'), may hold values from -6 to 6
- tile_column: int32 [256, 4, 8], P('row', 'col'), may hold values from 0 to 63
- tile_live: int32 [256, 4, 8], P('row', 'col'), may hold values 0 or 1
Outputs:
- orthonormal: float32 [64, 16384], P(None, ('row', 'col'))
- quotient: float32 [64, 64], replicated
All inputs are finite; a program needn't handle non-finite values. No bound on the sum of `tile_live` on one device may be relied on, other than what follows from the above.
Results may differ from a plain program's by a relative error of at most 0.0032.
Values may be sent and summed in bfloat16 or wider, within the bound.
No kernel may reach another device: no remote copies, remote signals or barrier semaphores. Data moves between devices by JAX's collectives and lax.ppermute only.
A program may use at most 128 MiB of HBM per device.

v0:
```python
import math
import jax
import jax.numpy as jnp
from jax import lax
from jax.sharding import PartitionSpec as P


def gram_of(left, right):
    return lax.dot_general(
        left,
        right,
        (((1,), (1,)), ((), ())),
        precision=lax.Precision.HIGHEST,
        preferred_element_type=jnp.float32,
    )


def on_device(krylov_block, degree, tile_values, tile_column, tile_live):
    vectors = krylov_block.shape[0]
    owned_rows = krylov_block.shape[1]
    block_rows = tile_values.shape[0]
    height = tile_values.shape[2]
    slot_width = tile_values.shape[3]
    sources = lax.axis_size("row")
    groups = lax.axis_size("col")
    per_piece = owned_rows // height
    inv_root = lax.rsqrt(degree.astype(jnp.float32))
    basis_wide = krylov_block.astype(jnp.float32)
    scaled = (basis_wide * inv_root[None, :]).astype(jnp.bfloat16)
    gathered = lax.all_gather(scaled, "row", axis=1, tiled=True)
    blocks = gathered.reshape(vectors, sources * per_piece, height)
    pick_index = tile_column[:, 0, :].reshape(-1)
    chosen = jnp.take(blocks, pick_index, axis=1)
    chosen = chosen * tile_live[:, 0, :].reshape(1, -1, 1).astype(jnp.bfloat16)
    chosen = chosen.reshape(vectors, block_rows, slot_width)
    panel = tile_values[:, 0]
    whole_rows = jnp.einsum("klc,luc->klu", chosen, panel, preferred_element_type=jnp.float32)
    whole_rows = whole_rows.reshape(vectors, block_rows * height)
    spread = lax.psum_scatter(whole_rows, "col", scatter_dimension=1, tiled=True)
    applied = basis_wide - inv_root[None, :] * spread
    quotient, energy = lax.psum(
        (gram_of(basis_wide, applied), gram_of(applied, applied)), ("row", "col")
    )
    factor = jnp.linalg.cholesky(energy)
    identity = jnp.eye(vectors, dtype=jnp.float32)
    inverse = lax.linalg.triangular_solve(factor, identity, left_side=True, lower=True)
    total_rows = sources * groups * owned_rows
    orthonormal = jnp.dot(inverse, applied, precision=lax.Precision.HIGHEST) * math.sqrt(total_rows)
    return (orthonormal, quotient / total_rows)


def solution(mesh):
    return jax.shard_map(
        on_device,
        mesh=mesh,
        in_specs=(
            P(None, ("row", "col")),
            P(("row", "col")),
            P("row", "col", None, None),
            P("row", "col", None),
            P("row", "col", None),
        ),
        out_specs=(P(None, ("row", "col")), P()),
        check_vma=False,
    )
```

profile of v0, /device:TPU:0, one launch (start us, length us, event | category | flops | bytes accessed | tf_op | source)
XLA Modules:
  0.0 156.6 jit_solution(8631686106743871151)
XLA Ops:
  7.2 0.0 copy-start
  7.2 0.0 reduce-scatter.2.cloned.1.call-start
  7.2 0.9 copy.22
  8.1 0.7 compare_and_fusion
  8.8 0.7 convert_rsqrt_fusion
  9.5 0.9 fusion.8
  10.4 33.0 %all_gather.3 = bf16[64,4096]{1,0:T(8,128)(2,1)S(1)} all-gather(bf16[64,512]{1,0:T(8,128)(2,1)S(1)} %fusion.8), channel_id=1, replica_groups=mesh['row'=8,'col'=4] {'row'}, dimensions={1}, use_global_device_ids=true | all-gather | bytes 589824 | tf_op jit(solution)/shard_map/all_gather | solution.py:30
  43.4 2.1 %reshape.72 = bf16[64,64,64]{2,1,0:T(8,128)(2,1)} reshape(bf16[64,4096]{1,0:T(8,128)(2,1)S(1)} %all_gather.3) | data formatting | bytes 1048576 | tf_op jit(solution)/shard_map/reshape | solution.py:31
  45.5 1.9 %copy.23 = bf16[64,64,64]{2,0,1:T(8,128)(2,1)S(1)} copy(bf16[64,64,64]{2,1,0:T(8,128)(2,1)} %reshape.72) | data formatting | bytes 1048576 | tf_op jit(solution)/shard_map/reshape | solution.py:31
  47.4 0.1 reshape_squeeze.7
  47.5 3.1 %gather_fusion = bf16[256,64,64]{2,1,0:T(8,128)(2,1)} fusion(bf16[64,64,64]{2,0,1:T(8,128)(2,1)S(1)} %copy.23, s32[1024]{0:T(1024)S(1)} %pad_clamp_fusion), kind=kCustom, calls=%fused_computation | custom fusion | bytes 4195328 | tf_op jit(solution)/shard_map/jit(_take)/gather | solution.py:33
  50.6 6.8 %copy.24 = bf16[64,256,64]{2,1,0:T(8,128)(2,1)} copy(bf16[64,256,64]{2,0,1:T(8,128)(2,1)} %bitcast.30) | data formatting | bytes 4194304 | tf_op jit(solution)/shard_map/jit(_take)/gather | solution.py:33
  57.4 0.0 copy-start.2
  57.4 6.5 %gather.7 = bf16[64,32,512]{2,1,0:T(8,128)(2,1)} reshape(bf16[64,256,64]{2,1,0:T(8,128)(2,1)} %copy.24) | data formatting | bytes 4194304 | tf_op jit(solution)/shard_map/jit(_take)/gather | solution.py:33
  63.9 0.0 copy-done.2
  63.9 0.1 copy.25
  64.0 0.1 mul.35
  64.1 0.1 mul.36
  64.2 0.1 copy.21
  64.3 0.1 broadcast_in_dim.18
  64.4 0.1 broadcast_in_dim.19
  64.5 1.8 %select_multiply_fusion = bf16[64,32,512]{2,1,0:T(8,128)(2,1)S(1)} fusion(bf16[64,32,512]{2,1,0:T(8,128)(2,1)} %gather.7, pred[32,512]{1,0:T(8,128)(4,1)S(1)} %broadcast_in_dim.19, bf16[32,512]{1,0:T(8,128)(2,1)S(1)} %mul.36), kind=kLoop, calls=%fused_computation.4 | loop fusion | flops 2097152 | bytes 4243456 | tf_op jit(solution)/shard_map/mul | solution.py:34
  66.3 0.0 copy-done
  66.3 1.4 fusion.3
  67.7 0.0 copy-start.1
  67.7 0.6 copy.27
  68.4 1.1 reshape.73
  69.5 0.0 reduce-scatter.2.cloned.1.call-update
  69.5 22.9 %reduce-scatter.2.cloned.1.call-done = f32[64,512]{1,0:T(8,128)} async-done(((f32[64,2048]{1,0:T(8,128)}), f32[64,512]{1,0:T(8,128)}) %reduce-scatter.2.cloned.1.call-update) | async-done | bytes 131088 | tf_op jit(solution)/shard_map/reduce_scatter | solution.py:39
  92.5 0.0 copy-done.1
  92.5 1.1 convolution_bitcast_fusion
  93.6 1.3 fusion.9
  94.8 40.0 %all-reduce = (f32[64,64]{0,1:T(8,128)S(1)}, f32[64,64]{0,1:T(8,128)S(1)}) all-reduce(f32[64,64]{0,1:T(8,128)S(1)} %fusion.9, f32[64,64]{0,1:T(8,128)S(1)} %convolution_bitcast_fusion), channel_id=1, replica_groups=mesh['row'=8,'col'=4] {'row','col'}, use_global_device_ids=true, to_apply=%region_1.2 | all-reduce | flops 8192 | bytes 65536 | tf_op jit(solution)/shard_map/psum | solution.py:41
  134.8 0.1 copy.29
  134.9 5.8 %cholesky.17 = f32[64,64]{1,0:T(8,128)S(1)} custom-call(f32[64,64]{1,0:T(8,128)S(1)} %fusion.16), custom_call_target="Cholesky" | custom-call | tf_op jit(solution)/shard_map/jit(cholesky)/cholesky | solution.py:44
  140.8 0.6 compare_reduce_fusion
  141.4 0.7 fusion.13
  142.1 4.9 %custom-call.6 = f32[1,64,64]{1,2,0:T(8,128)S(1)} custom-call(f32[1,64,64]{2,1,0:T(8,128)S(1)} %fusion.13), custom_call_target="InvertDiagBlocksLowerTriangular" | custom-call | tf_op jit(solution)/shard_map/triangular_solve | solution.py:46
  147.0 0.2 fusion.14
  147.3 0.7 copy.30
  148.0 1.8 %convolution_multiply_fusion = f32[64,512]{1,0:T(8,128)} fusion(f32[64,64]{1,0:T(8,128)S(1)} %fusion.14, bf16[64,512]{1,0:T(8,128)(2,1)S(1)} %copy-done.1, f32[64,512]{1,0:T(8,128)} %reduce-scatter.2.cloned.1.call-done, f32[512]{0:T(512)S(1)} %convert_rsqrt_fusion), kind=kOutput, calls=%fused_computation.6 | convolution fusion | flops 25296896 | bytes 346112 | tf_op jit(solution)/shard_map/dot_general | solution.py:48
  (6 shorter events, 0.1 us)
Async XLA Ops:
  7.2 59.1 %copy-start = (bf16[32,1,64,512]{3,2,1,0:T(8,128)(2,1)S(1)}, bf16[32,1,64,512]{3,2,1,0:T(8,128)(2,1)}, u32[]{:S(2)}) copy-start(bf16[32,1,64,512]{3,2,1,0:T(8,128)(2,1)} %param.7) | copy-start | bytes 6291460
  7.2 85.3 %reduce-scatter.2.cloned.1.call-start = ((), (), s32[]{:S(2)}) async-start(), calls=%async_computation.1 | async-start | bytes 655360 | tf_op jit(solution)/shard_map/reduce_scatter | solution.py:39
  57.4 6.5 %copy-start.2 = (s32[32,1,8]{0,2,1:T(8,128)S(1)}, s32[32,1,8]{0,2,1:T(8,128)}, u32[]{:S(2)}) copy-start(s32[32,1,8]{0,2,1:T(8,128)} %param.9) | copy-start | bytes 3076
  67.7 24.7 %copy-start.1 = (bf16[64,512]{1,0:T(8,128)(2,1)S(1)}, bf16[64,512]{1,0:T(8,128)(2,1)}, u32[]{:S(2)}) copy-start(bf16[64,512]{1,0:T(8,128)(2,1)} %param.5) | copy-start | bytes 196612
Sparse Core Ops, SparseCore 0:
  69.7 22.7 reduce-scatter.1
where the time goes:
time: 157 us
  blocking collectives  73 us (46%)
  local copies, waits for them, and re-layouts  24.5 us (16%)
  waiting for transfers between devices  22.9 us (15%)
  other arithmetic  16.1 us (10%)
  between operations  14.1 us (9%)
  matrix products  5.85 us (4%)
    psum x1, blocking collectives, on_device(): lax.psum((gram_of(basis_wide, applied), gram_of(applied, applied)), ('row...  40 us
    all_gather x1, blocking collectives, on_device(): gathered = lax.all_gather(scaled, 'row', axis=1, tiled=True)  33 us
    reduce_scatter x1, waiting for transfers between devices, on_device(): lax.psum_scatter(whole_rows, 'col', scatter_dimension=1, tiled=True)  22.9 us
    gather x3, local copies, waits for them, and re-layouts, on_device(): chosen = jnp.take(blocks, pick_index, axis=1)  16.3 us
    another operation x3, other arithmetic, on_device(): factor = jnp.linalg.cholesky(energy)  6.52 us
    another operation x2, other arithmetic, on_device(): lax.linalg.triangular_solve(factor, identity, left_side=True, lower=True)  5.55 us
    reshape x2, local copies, waits for them, and re-layouts, on_device(): blocks = gathered.reshape(vectors, sources * per_piece, height)  4.01 us
  transfers between devices with their start and end apart: 1, of which 1 were waited for; matrix products, arithmetic and copies ran while one was open for 0% of the time, Pallas kernels for 0%

commit v1 on v0

--- a/solution.py
+++ b/solution.py
@@ -39,7 +39,7 @@
     spread = lax.psum_scatter(whole_rows, "col", scatter_dimension=1, tiled=True)
     applied = basis_wide - inv_root[None, :] * spread
     quotient, energy = lax.psum(
-        (gram_of(basis_wide, applied), gram_of(applied, applied)), ("row", "col")
+        lax.psum((gram_of(basis_wide, applied), gram_of(applied, applied)), "col"), "row"
     )
     factor = jnp.linalg.cholesky(energy)
     identity = jnp.eye(vectors, dtype=jnp.float32)

time: 157 us -> 166 us (1.057)
  blocking collectives: 73 us -> 81.6 us
    psum x1 -> x2, blocking collectives: 40 us -> 48.6 us  [the longest x1 37.8 us: on_device(): lax.psum(lax.psum((gram_of(basis_wide, applied), gram_of(applied, applied...]
where the time goes in v1:
time: 166 us; the launch traced here: 165 us
  blocking collectives  81.6 us (49%)
  local copies, waits for them, and re-layouts  24.5 us (15%)
  waiting for transfers between devices  22.9 us (14%)
  other arithmetic  16.1 us (10%)
  between operations  14.2 us (9%)
  matrix products  5.85 us (4%)
    psum x1, blocking collectives, on_device(): lax.psum(lax.psum((gram_of(basis_wide, applied), gram_of(applied, applied...  37.8 us
    all_gather x1, blocking collectives, on_device(): gathered = lax.all_gather(scaled, 'row', axis=1, tiled=True)  33 us
    reduce_scatter x1, waiting for transfers between devices, on_device(): lax.psum_scatter(whole_rows, 'col', scatter_dimension=1, tiled=True)  22.9 us
    gather x3, local copies, waits for them, and re-layouts, on_device(): chosen = jnp.take(blocks, pick_index, axis=1)  16.3 us
    psum x1, blocking collectives, on_device(): lax.psum((gram_of(basis_wide, applied), gram_of(applied, applied)), 'col')  10.7 us
    another operation x3, other arithmetic, on_device(): factor = jnp.linalg.cholesky(energy)  6.52 us
    another operation x2, other arithmetic, on_device(): lax.linalg.triangular_solve(factor, identity, left_side=True, lower=True)  5.55 us
    reshape x2, local copies, waits for them, and re-layouts, on_device(): blocks = gathered.reshape(vectors, sources * per_piece, height)  4.01 us
  transfers between devices with their start and end apart: 1, of which 1 were waited for; matrix products, arithmetic and copies ran while one was open for 0% of the time, Pallas kernels for 0%

profile of v1, /device:TPU:0, one launch (start us, length us, event | category | flops | bytes accessed | tf_op | source)
XLA Modules:
  0.0 165.2 jit_solution(10301611805834197570)
XLA Ops:
  7.2 0.0 copy-start
  7.2 0.0 reduce-scatter.2.cloned.1.call-start
  7.2 0.9 copy.22
  8.1 0.7 compare_and_fusion
  8.8 0.7 convert_rsqrt_fusion
  9.5 0.9 fusion.8
  10.4 33.0 %all_gather.3 = bf16[64,4096]{1,0:T(8,128)(2,1)S(1)} all-gather(bf16[64,512]{1,0:T(8,128)(2,1)S(1)} %fusion.8), channel_id=1, replica_groups=mesh['row'=8,'col'=4] {'row'}, dimensions={1}, use_global_device_ids=true | all-gather | bytes 589824 | tf_op jit(solution)/shard_map/all_gather | solution.py:30
  43.4 2.1 %reshape.72 = bf16[64,64,64]{2,1,0:T(8,128)(2,1)} reshape(bf16[64,4096]{1,0:T(8,128)(2,1)S(1)} %all_gather.3) | data formatting | bytes 1048576 | tf_op jit(solution)/shard_map/reshape | solution.py:31
  45.5 1.9 %copy.23 = bf16[64,64,64]{2,0,1:T(8,128)(2,1)S(1)} copy(bf16[64,64,64]{2,1,0:T(8,128)(2,1)} %reshape.72) | data formatting | bytes 1048576 | tf_op jit(solution)/shard_map/reshape | solution.py:31
  47.4 0.1 reshape_squeeze.7
  47.5 3.1 %gather_fusion = bf16[256,64,64]{2,1,0:T(8,128)(2,1)} fusion(bf16[64,64,64]{2,0,1:T(8,128)(2,1)S(1)} %copy.23, s32[1024]{0:T(1024)S(1)} %pad_clamp_fusion), kind=kCustom, calls=%fused_computation | custom fusion | bytes 4195328 | tf_op jit(solution)/shard_map/jit(_take)/gather | solution.py:33
  50.6 6.8 %copy.24 = bf16[64,256,64]{2,1,0:T(8,128)(2,1)} copy(bf16[64,256,64]{2,0,1:T(8,128)(2,1)} %bitcast.30) | data formatting | bytes 4194304 | tf_op jit(solution)/shard_map/jit(_take)/gather | solution.py:33
  57.4 0.0 copy-start.2
  57.4 6.5 %gather.7 = bf16[64,32,512]{2,1,0:T(8,128)(2,1)} reshape(bf16[64,256,64]{2,1,0:T(8,128)(2,1)} %copy.24) | data formatting | bytes 4194304 | tf_op jit(solution)/shard_map/jit(_take)/gather | solution.py:33
  63.9 0.0 copy-done.2
  63.9 0.1 copy.25
  64.0 0.1 mul.35
  64.1 0.1 mul.36
  64.2 0.1 copy.21
  64.3 0.1 broadcast_in_dim.18
  64.4 0.1 broadcast_in_dim.19
  64.5 1.8 %select_multiply_fusion = bf16[64,32,512]{2,1,0:T(8,128)(2,1)S(1)} fusion(bf16[64,32,512]{2,1,0:T(8,128)(2,1)} %gather.7, pred[32,512]{1,0:T(8,128)(4,1)S(1)} %broadcast_in_dim.19, bf16[32,512]{1,0:T(8,128)(2,1)S(1)} %mul.36), kind=kLoop, calls=%fused_computation.4 | loop fusion | flops 2097152 | bytes 4243456 | tf_op jit(solution)/shard_map/mul | solution.py:34
  66.3 0.0 copy-done
  66.3 1.4 fusion.3
  67.7 0.0 copy-start.1
  67.7 0.6 copy.27
  68.4 1.1 reshape.73
  69.5 0.0 reduce-scatter.2.cloned.1.call-update
  69.5 22.9 %reduce-scatter.2.cloned.1.call-done = f32[64,512]{1,0:T(8,128)} async-done(((f32[64,2048]{1,0:T(8,128)}), f32[64,512]{1,0:T(8,128)}) %reduce-scatter.2.cloned.1.call-update) | async-done | bytes 131088 | tf_op jit(solution)/shard_map/reduce_scatter | solution.py:39
  92.5 0.0 copy-done.1
  92.5 1.1 convolution_bitcast_fusion
  93.6 1.3 fusion.9
  94.8 10.7 %all-reduce.1 = (f32[64,64]{0,1:T(8,128)S(1)}, f32[64,64]{0,1:T(8,128)S(1)}) all-reduce(f32[64,64]{0,1:T(8,128)S(1)} %fusion.9, f32[64,64]{0,1:T(8,128)S(1)} %convolution_bitcast_fusion), channel_id=1, replica_groups=mesh['row'=8,'col'=4] {'col'}, use_global_device_ids=true, to_apply=%region_1.2 | all-reduce | flops 8192 | bytes 65536 | tf_op jit(solution)/shard_map/psum | solution.py:42
  105.6 37.8 %all-reduce = (f32[64,64]{0,1:T(8,128)S(1)}, f32[64,64]{0,1:T(8,128)S(1)}) all-reduce(f32[64,64]{0,1:T(8,128)S(1)} %get-tuple-element.10, f32[64,64]{0,1:T(8,128)S(1)} %get-tuple-element.11), channel_id=1, replica_groups=mesh['row'=8,'col'=4] {'row'}, use_global_device_ids=true, to_apply=%region_2.3 | all-reduce | flops 8192 | bytes 65536 | tf_op jit(solution)/shard_map/psum | solution.py:41
  143.4 0.1 copy.29
  143.5 5.8 %cholesky.17 = f32[64,64]{1,0:T(8,128)S(1)} custom-call(f32[64,64]{1,0:T(8,128)S(1)} %fusion.16), custom_call_target="Cholesky" | custom-call | tf_op jit(solution)/shard_map/jit(cholesky)/cholesky | solution.py:44
  149.4 0.6 compare_reduce_fusion
  150.0 0.7 fusion.13
  150.7 4.9 %custom-call.6 = f32[1,64,64]{1,2,0:T(8,128)S(1)} custom-call(f32[1,64,64]{2,1,0:T(8,128)S(1)} %fusion.13), custom_call_target="InvertDiagBlocksLowerTriangular" | custom-call | tf_op jit(solution)/shard_map/triangular_solve | solution.py:46
  155.6 0.2 fusion.14
  155.8 0.7 copy.30
  156.5 1.8 %convolution_multiply_fusion = f32[64,512]{1,0:T(8,128)} fusion(f32[64,64]{1,0:T(8,128)S(1)} %fusion.14, bf16[64,512]{1,0:T(8,128)(2,1)S(1)} %copy-done.1, f32[64,512]{1,0:T(8,128)} %reduce-scatter.2.cloned.1.call-done, f32[512]{0:T(512)S(1)} %convert_rsqrt_fusion), kind=kOutput, calls=%fused_computation.6 | convolution fusion | flops 25296896 | bytes 346112 | tf_op jit(solution)/shard_map/dot_general | solution.py:48
  (6 shorter events, 0.1 us)
Async XLA Ops:
  7.2 59.1 %copy-start = (bf16[32,1,64,512]{3,2,1,0:T(8,128)(2,1)S(1)}, bf16[32,1,64,512]{3,2,1,0:T(8,128)(2,1)}, u32[]{:S(2)}) copy-start(bf16[32,1,64,512]{3,2,1,0:T(8,128)(2,1)} %param.7) | copy-start | bytes 6291460
  7.2 85.3 %reduce-scatter.2.cloned.1.call-start = ((), (), s32[]{:S(2)}) async-start(), calls=%async_computation.1 | async-start | bytes 655360 | tf_op jit(solution)/shard_map/reduce_scatter | solution.py:39
  57.4 6.5 %copy-start.2 = (s32[32,1,8]{0,2,1:T(8,128)S(1)}, s32[32,1,8]{0,2,1:T(8,128)}, u32[]{:S(2)}) copy-start(s32[32,1,8]{0,2,1:T(8,128)} %param.9) | copy-start | bytes 3076
  67.7 24.7 %copy-start.1 = (bf16[64,512]{1,0:T(8,128)(2,1)S(1)}, bf16[64,512]{1,0:T(8,128)(2,1)}, u32[]{:S(2)}) copy-start(bf16[64,512]{1,0:T(8,128)(2,1)} %param.5) | copy-start | bytes 196612
Sparse Core Ops, SparseCore 0:
  69.7 22.7 reduce-scatter.1
